TPU v7x, 256 devices: a whole 4x4x8 slice. The times are simulated.
256 devices in a mesh: coarse: 8 (over z), fine: 32 (over x, y, core).
Axes of the slice: x: 4, y: 4, z: 8, core: 2. Of those that a mesh axis runs over, the one named last changes fastest.
Arguments:
- volume: float32 [2048, 256, 1024], P(('coarse', 'fine')), may hold values from -6 to 6
- color_params: float32 [2, 3], replicated, may hold values from -2 to 2
- depth_order: int32 [8], replicated, may hold values from 0 to 7, each once
Outputs:
- final_image: float32 [3, 256, 1024], P(None, 'fine', 'coarse')
- opacity: float32 [256, 1024], P('fine', 'coarse')
Inputs may be any that keep to these rules, and one draw needn't show every extreme that they name: `depth_order`: every place 0 to 7 is held by exactly one group.
All inputs are finite; a program needn't handle non-finite values.
Results may differ from a plain program's by a relative error of at most 0.0001.
Values sent between devices are 32-bit elements; how exact they have to be, the bound alone decides.
A program may use at most 64 MiB of HBM per device.

v0:
```python
import jax
import jax.numpy as jnp
from jax import lax
from jax.sharding import PartitionSpec as P


def padded_2(block, sides, width):
    for axis, dim in sides:
        count = lax.axis_size(axis)
        forward = [(i, i + 1) for i in range(count - 1)]
        backward = [(target, source) for source, target in forward]
        low = lax.ppermute(
            lax.slice_in_dim(block, block.shape[dim] - width, None, axis=dim), axis, forward
        )
        high = lax.ppermute(lax.slice_in_dim(block, 0, width, axis=dim), axis, backward)
        block = jnp.concatenate([low, block, high], axis=dim)
    return block


def plane_terms(previous_plane, centre_plane, next_plane, color_params, sample_step):
    grad_depth = 0.5 * (next_plane - previous_plane)
    row_padded = jnp.concatenate([centre_plane[:1], centre_plane, centre_plane[-1:]], axis=0)
    grad_row = 0.5 * (row_padded[2:] - row_padded[:-2])
    col_padded = jnp.concatenate([centre_plane[:, :1], centre_plane, centre_plane[:, -1:]], axis=1)
    grad_col = 0.5 * (col_padded[:, 2:] - col_padded[:, :-2])
    lit_term = (2.0 * grad_depth + grad_row + 2.0 * grad_col) / 3.0
    norm_term = jnp.sqrt(grad_depth * grad_depth + grad_row * grad_row + grad_col * grad_col + 1.0)
    shading = 0.35 + 0.65 * jnp.abs(lit_term) / norm_term
    slopes = color_params[0][:, None, None]
    offsets = color_params[1][:, None, None]
    emitted = 3.0 * shading[None] * jax.nn.sigmoid(slopes * centre_plane[None] + offsets)
    optical = 0.25 * centre_plane * centre_plane * sample_step
    return (emitted, optical)


def march_slab(padded, color_params, sample_step, radiance, depth_sum):
    plane_count = padded.shape[0] - 2

    def advance(plane_index, state_pair):
        radiance_now, depth_now = state_pair
        previous_plane = lax.dynamic_index_in_dim(padded, plane_index, 0, keepdims=False)
        centre_plane = lax.dynamic_index_in_dim(padded, plane_index + 1, 0, keepdims=False)
        next_plane = lax.dynamic_index_in_dim(padded, plane_index + 2, 0, keepdims=False)
        emitted, optical = plane_terms(
            previous_plane, centre_plane, next_plane, color_params, sample_step
        )
        weight = jnp.exp(-depth_now) * -jnp.expm1(-optical)
        return (radiance_now + weight[None] * emitted, depth_now + optical)

    return lax.fori_loop(0, plane_count, advance, (radiance, depth_sum))


def body(volume, color_params, depth_order):
    depth_dev, row_count, col_count = volume.shape
    fine_count = lax.axis_size("fine")
    coarse_count = lax.axis_size("coarse")
    fine_index = lax.axis_index("fine")
    sample_step = 4.0 / (depth_dev * coarse_count * fine_count)
    padded = padded_2(volume, (("fine", 0),), 1)
    lower_plane = jnp.where(fine_index == 0, volume[0], padded[0])
    upper_plane = jnp.where(fine_index == fine_count - 1, volume[-1], padded[-1])
    padded = jnp.concatenate([lower_plane[None], volume, upper_plane[None]], axis=0)
    empty_rad = jnp.zeros((3, row_count, col_count), jnp.float32)
    empty_depth = jnp.zeros((row_count, col_count), jnp.float32)
    radiance, depth_sum = march_slab(padded, color_params, sample_step, empty_rad, empty_depth)
    row_block = row_count // fine_count
    radiance = radiance.reshape(3, fine_count, row_block, col_count)
    log_trans = (-depth_sum).reshape(1, fine_count, row_block, col_count)
    got_rad, got_log = (
        lax.all_to_all(radiance, "fine", split_axis=1, concat_axis=1, tiled=True),
        lax.all_to_all(log_trans, "fine", split_axis=1, concat_axis=1, tiled=True),
    )
    before_sum = jnp.cumsum(got_log, axis=1) - got_log
    radiance = jnp.sum(jnp.exp(before_sum) * got_rad, axis=1)
    log_trans = jnp.sum(got_log, axis=1)
    col_block = col_count // coarse_count
    radiance = radiance.reshape(3, row_block, coarse_count, col_block)
    log_trans = log_trans.reshape(1, row_block, coarse_count, col_block)
    got_rad, got_log = (
        lax.all_to_all(radiance, "coarse", split_axis=2, concat_axis=2, tiled=True),
        lax.all_to_all(log_trans, "coarse", split_axis=2, concat_axis=2, tiled=True),
    )
    before_mask = (depth_order[None, :] < depth_order[:, None]).astype(jnp.float32)
    before_sum = jnp.einsum("gh,crhw->crgw", before_mask, got_log, precision=lax.Precision.HIGHEST)
    final_image = jnp.sum(jnp.exp(before_sum) * got_rad, axis=2)
    opacity = -jnp.expm1(jnp.sum(got_log, axis=2))[0]
    return (final_image, opacity)


def solution(mesh):
    return jax.shard_map(
        body,
        mesh=mesh,
        in_specs=(P(("coarse", "fine"), None, None), P(), P()),
        out_specs=(P(None, "fine", "coarse"), P("fine", "coarse")),
        check_vma=False,
    )
```

profile of v0, /device:TPU:1, one launch (start us, length us, event | category | flops | bytes accessed | tf_op | source)
XLA Modules:
  0.0 213.2 jit_solution(619306491763541161)
XLA Ops:
  0.6 2.7 %fusion.30 = (f32[1,256,1024]{2,1,0:T(8,128)}, f32[1,256,1024]{2,1,0:T(8,128)S(1)}) fusion(f32[8,256,1024]{2,1,0:T(8,128)} %param.5), kind=kLoop, calls=%fused_computation.52 | loop fusion | bytes 4194304 | tf_op jit(solution)/shard_map/slice | solution.py:13
  3.3 4.6 %collective-permute-start = (f32[1,256,1024]{2,1,0:T(8,128)}, f32[1,256,1024]{2,1,0:T(8,128)S(1)}, u32[]{:S(2)}, u32[]{:S(2)}) collective-permute-start(f32[1,256,1024]{2,1,0:T(8,128)} %get-tuple-element.199), channel_id=1, source_target_pairs={{0,1},{1,2},{2,3},{3,4},{4,5},{5,6},{6,7},{7,8},{8,9},{9,10},{10,1... | collective-permute-start | bytes 3145736 | tf_op jit(solution)/shard_map/ppermute | solution.py:12
  9.9 10.1 %collective-permute-done = f32[1,256,1024]{2,1,0:T(8,128)S(1)} collective-permute-done((f32[1,256,1024]{2,1,0:T(8,128)}, f32[1,256,1024]{2,1,0:T(8,128)S(1)}, u32[]{:S(2)}, u32[]{:S(2)}) %collective-permute-start) | collective-permute-done | bytes 1048608 | tf_op jit(solution)/shard_map/ppermute | solution.py:12
  20.0 4.2 %collective-permute-done.1 = f32[1,256,1024]{2,1,0:T(8,128)} collective-permute-done((f32[1,256,1024]{2,1,0:T(8,128)S(1)}, f32[1,256,1024]{2,1,0:T(8,128)}, u32[]{:S(2)}, u32[]{:S(2)}) %collective-permute-start.1) | collective-permute-done | bytes 1048608 | tf_op jit(solution)/shard_map/ppermute | solution.py:15
  24.1 2.3 %broadcast_select_fusion.1 = (f32[1,256,1024]{2,1,0:T(8,128)S(1)}, f32[1,256,1024]{2,1,0:T(8,128)S(1)}) fusion(f32[1,256,1024]{2,1,0:T(8,128)S(1)} %collective-permute-done, pred[]{:T(512)S(6)} %eq.6, f32[8,256,1024]{2,1,0:T(8,128)} %param.5, f32[1,256,1024]{2,1,0:T(8,128)} %collective-permute-done.1, pred[]{:T(512)S(6)} %eq.7), kind=kLoop, calls=%fused_computation.41 | loop fusion | flops 524288 | bytes 6291458 | tf_op jit(solution)/shard_map/jit(_where)/select_n | solution.py:60
  26.5 9.6 %pad_maximum_fusion.4 = f32[10,256,1024]{2,1,0:T(8,128)} fusion(f32[1,256,1024]{2,1,0:T(8,128)S(1)} %get-tuple-element.198, f32[8,256,1024]{2,1,0:T(8,128)} %param.5, f32[1,256,1024]{2,1,0:T(8,128)S(1)} %get-tuple-element.197), kind=kLoop, calls=%fused_computation.31 | loop fusion | flops 5242880 | bytes 20971520 | tf_op jit(solution)/shard_map/concatenate | solution.py:62
  36.1 76.0 %while.19 = (s32[]{:T(128)}, f32[3,256,1024]{2,1,0:T(8,128)}, f32[256,1024]{1,0:T(8,128)S(1)}, f32[10,256,1024]{2,1,0:T(8,128)}, f32[2,3]{1,0:T(2,128)S(1)}, /*i...) while((s32[]{:T(128)}, f32[3,256,1024]{2,1,0:T(8,128)}, ...), condition=%wide.region_1.2_spmd.clone, body=%wide.region_0.1_spmd.clone.sunk | while | flops 16777228 | bytes 47217004 | solution.py:50
  38.5 3.2 %negate_multiply_fusion.2 = (f32[256,1024]{1,0:T(8,128)S(1)}, f32[256,1024]{1,0:T(8,128)S(1)}) fusion(f32[256,1024]{1,0:T(8,128)S(1)} %get-tuple-element.265, f32[256,1024]{1,0:T(8,128)S(1)} %get-tuple-element.243, pred[]{:T(512)S(6)} %compare.3, f32[256,1]{1,0:T(8,128)S(1)} %get-tuple-element.245, f32[256,1]{1,0:T(8,128)S(1)} %get-tuple-element.246, ...), kind=kLoop, calls=%fused_computation.24.clone.1 | loop fusion | flops 8388608 | bytes 6301705 | tf_op jit(solution)/shard_map/while/body/eval_jaxpr/mul | solution.py:47
  41.8 2.0 select_add_fusion.5
  48.0 3.2 %negate_multiply_fusion.2 = (f32[256,1024]{1,0:T(8,128)S(1)}, f32[256,1024]{1,0:T(8,128)S(1)}) fusion(f32[256,1024]{1,0:T(8,128)S(1)} %get-tuple-element.265, f32[256,1024]{1,0:T(8,128)S(1)} %get-tuple-element.243, pred[]{:T(512)S(6)} %compare.3, f32[256,1]{1,0:T(8,128)S(1)} %get-tuple-element.245, f32[256,1]{1,0:T(8,128)S(1)} %get-tuple-element.246, ...), kind=kLoop, calls=%fused_computation.24.clone.1 | loop fusion | flops 8388608 | bytes 6301705 | tf_op jit(solution)/shard_map/while/body/eval_jaxpr/mul | solution.py:47
  51.3 2.0 select_add_fusion.5
  57.5 3.2 %negate_multiply_fusion.2 = (f32[256,1024]{1,0:T(8,128)S(1)}, f32[256,1024]{1,0:T(8,128)S(1)}) fusion(f32[256,1024]{1,0:T(8,128)S(1)} %get-tuple-element.265, f32[256,1024]{1,0:T(8,128)S(1)} %get-tuple-element.243, pred[]{:T(512)S(6)} %compare.3, f32[256,1]{1,0:T(8,128)S(1)} %get-tuple-element.245, f32[256,1]{1,0:T(8,128)S(1)} %get-tuple-element.246, ...), kind=kLoop, calls=%fused_computation.24.clone.1 | loop fusion | flops 8388608 | bytes 6301705 | tf_op jit(solution)/shard_map/while/body/eval_jaxpr/mul | solution.py:47
  60.8 2.0 select_add_fusion.5
  67.0 3.2 %negate_multiply_fusion.2 = (f32[256,1024]{1,0:T(8,128)S(1)}, f32[256,1024]{1,0:T(8,128)S(1)}) fusion(f32[256,1024]{1,0:T(8,128)S(1)} %get-tuple-element.265, f32[256,1024]{1,0:T(8,128)S(1)} %get-tuple-element.243, pred[]{:T(512)S(6)} %compare.3, f32[256,1]{1,0:T(8,128)S(1)} %get-tuple-element.245, f32[256,1]{1,0:T(8,128)S(1)} %get-tuple-element.246, ...), kind=kLoop, calls=%fused_computation.24.clone.1 | loop fusion | flops 8388608 | bytes 6301705 | tf_op jit(solution)/shard_map/while/body/eval_jaxpr/mul | solution.py:47
  70.3 2.0 select_add_fusion.5
  76.5 3.2 %negate_multiply_fusion.2 = (f32[256,1024]{1,0:T(8,128)S(1)}, f32[256,1024]{1,0:T(8,128)S(1)}) fusion(f32[256,1024]{1,0:T(8,128)S(1)} %get-tuple-element.265, f32[256,1024]{1,0:T(8,128)S(1)} %get-tuple-element.243, pred[]{:T(512)S(6)} %compare.3, f32[256,1]{1,0:T(8,128)S(1)} %get-tuple-element.245, f32[256,1]{1,0:T(8,128)S(1)} %get-tuple-element.246, ...), kind=kLoop, calls=%fused_computation.24.clone.1 | loop fusion | flops 8388608 | bytes 6301705 | tf_op jit(solution)/shard_map/while/body/eval_jaxpr/mul | solution.py:47
  79.8 2.0 select_add_fusion.5
  86.0 3.2 %negate_multiply_fusion.2 = (f32[256,1024]{1,0:T(8,128)S(1)}, f32[256,1024]{1,0:T(8,128)S(1)}) fusion(f32[256,1024]{1,0:T(8,128)S(1)} %get-tuple-element.265, f32[256,1024]{1,0:T(8,128)S(1)} %get-tuple-element.243, pred[]{:T(512)S(6)} %compare.3, f32[256,1]{1,0:T(8,128)S(1)} %get-tuple-element.245, f32[256,1]{1,0:T(8,128)S(1)} %get-tuple-element.246, ...), kind=kLoop, calls=%fused_computation.24.clone.1 | loop fusion | flops 8388608 | bytes 6301705 | tf_op jit(solution)/shard_map/while/body/eval_jaxpr/mul | solution.py:47
  89.3 2.0 select_add_fusion.5
  95.5 3.2 %negate_multiply_fusion.2 = (f32[256,1024]{1,0:T(8,128)S(1)}, f32[256,1024]{1,0:T(8,128)S(1)}) fusion(f32[256,1024]{1,0:T(8,128)S(1)} %get-tuple-element.265, f32[256,1024]{1,0:T(8,128)S(1)} %get-tuple-element.243, pred[]{:T(512)S(6)} %compare.3, f32[256,1]{1,0:T(8,128)S(1)} %get-tuple-element.245, f32[256,1]{1,0:T(8,128)S(1)} %get-tuple-element.246, ...), kind=kLoop, calls=%fused_computation.24.clone.1 | loop fusion | flops 8388608 | bytes 6301705 | tf_op jit(solution)/shard_map/while/body/eval_jaxpr/mul | solution.py:47
  98.8 2.0 select_add_fusion.5
  105.0 3.2 %negate_multiply_fusion.2 = (f32[256,1024]{1,0:T(8,128)S(1)}, f32[256,1024]{1,0:T(8,128)S(1)}) fusion(f32[256,1024]{1,0:T(8,128)S(1)} %get-tuple-element.265, f32[256,1024]{1,0:T(8,128)S(1)} %get-tuple-element.243, pred[]{:T(512)S(6)} %compare.3, f32[256,1]{1,0:T(8,128)S(1)} %get-tuple-element.245, f32[256,1]{1,0:T(8,128)S(1)} %get-tuple-element.246, ...), kind=kLoop, calls=%fused_computation.24.clone.1 | loop fusion | flops 8388608 | bytes 6301705 | tf_op jit(solution)/shard_map/while/body/eval_jaxpr/mul | solution.py:47
  112.2 25.1 %all_to_all.20 = f32[1,32,8,1024]{3,2,0,1:T(8,128)S(1)} all-to-all(f32[1,32,8,1024]{3,2,0,1:T(8,128)S(1)} %negate_bitcast_fusion), channel_id=1, replica_groups=mesh['coarse'=8,'fine'=32] {'fine'}, dimensions={1} | all-to-all | bytes 2097152 | tf_op jit(solution)/shard_map/all_to_all | solution.py:71
  138.0 8.2 %all-to-all-start.1 = ((f32[1,8,8,128]{3,1,0,2:T(8,128)}), f32[1,8,8,128]{3,1,0,2:T(8,128)S(1)}, u32[]{:S(2)}, u32[]{:S(2)}) async-start(f32[1,8,8,128]{3,1,0,2:T(8,128)} %bitcast.1), calls=%async_computation.1 | async-start | bytes 65536 | tf_op jit(solution)/shard_map/all_to_all | solution.py:81
  146.2 4.0 %copy.13 = f32[3,32,8,1024]{3,2,0,1:T(8,128)} copy(f32[3,32,8,1024]{3,2,1,0:T(8,128)} %bitcast.78) | data formatting | bytes 6291456 | tf_op jit(solution)/shard_map/reshape | solution.py:67
  150.1 2.9 %all-to-all-done.1 = f32[1,8,8,128]{3,1,0,2:T(8,128)S(1)} async-done(((f32[1,8,8,128]{3,1,0,2:T(8,128)}), f32[1,8,8,128]{3,1,0,2:T(8,128)S(1)}, u32[]{:S(2)}, u32[]{:S(2)}) %all-to-all-start.1) | async-done | bytes 32800 | tf_op jit(solution)/shard_map/all_to_all | solution.py:81
  153.0 5.9 %all-to-all-start.2 = ((f32[3,32,8,1024]{3,2,0,1:T(8,128)}), f32[3,32,8,1024]{3,2,0,1:T(8,128)}, u32[]{:S(2)}, u32[]{:S(2)}) async-start(f32[3,32,8,1024]{3,2,0,1:T(8,128)} %copy.13), calls=%async_computation.2 | async-start | bytes 6291456 | tf_op jit(solution)/shard_map/all_to_all | solution.py:70
  159.0 16.1 %exponential_bitcast_fusion = f32[32,8,1024]{2,1,0:T(8,128)S(1)} fusion(f32[1,32,8,1024]{3,2,0,1:T(8,128)S(1)} %all_to_all.20), kind=kOutput, calls=%fused_computation.38 | output fusion | flops 8388608 | bytes 2097152 | tf_op jit(solution)/shard_map/jit(cumsum)/reduce_window_sum | solution.py:73
  175.3 23.6 %all-to-all-done.2 = f32[3,32,8,1024]{3,2,0,1:T(8,128)} async-done(((f32[3,32,8,1024]{3,2,0,1:T(8,128)}), f32[3,32,8,1024]{3,2,0,1:T(8,128)}, u32[]{:S(2)}, u32[]{:S(2)}) %all-to-all-start.2) | async-done | bytes 3145760 | tf_op jit(solution)/shard_map/all_to_all | solution.py:70
  198.9 2.3 %multiply_reduce_fusion = f32[3,8,1024]{2,1,0:T(8,128)S(1)} fusion(f32[3,32,8,1024]{3,2,0,1:T(8,128)} %all-to-all-done.2, f32[32,8,1024]{2,1,0:T(8,128)S(1)} %exponential_bitcast_fusion), kind=kLoop, calls=%fused_computation.32 | loop fusion | flops 1548288 | bytes 4292608 | tf_op jit(solution)/shard_map/reduce_sum | solution.py:74
  201.9 3.4 %all-to-all-start.3 = ((f32[3,8,8,128]{3,1,0,2:T(8,128)}), f32[3,8,8,128]{3,1,0,2:T(8,128)S(1)}, u32[]{:S(2)}, u32[]{:S(2)}) async-start(f32[3,8,8,128]{3,1,0,2:T(8,128)} %copy_bitcast_fusion), calls=%async_computation.3 | async-start | bytes 196608 | tf_op jit(solution)/shard_map/all_to_all | solution.py:80
  205.8 6.7 %all-to-all-done.3 = f32[3,8,8,128]{3,1,0,2:T(8,128)S(1)} async-done(((f32[3,8,8,128]{3,1,0,2:T(8,128)}), f32[3,8,8,128]{3,1,0,2:T(8,128)S(1)}, u32[]{:S(2)}, u32[]{:S(2)}) %all-to-all-start.3) | async-done | bytes 98336 | tf_op jit(solution)/shard_map/all_to_all | solution.py:80
  (88 shorter events, 40.5 us)
Async XLA Ops:
  3.3 16.6 %collective-permute-start = (f32[1,256,1024]{2,1,0:T(8,128)}, f32[1,256,1024]{2,1,0:T(8,128)S(1)}, u32[]{:S(2)}, u32[]{:S(2)}) collective-permute-start(f32[1,256,1024]{2,1,0:T(8,128)} %get-tuple-element.199), channel_id=1, source_target_pairs={{0,1},{1,2},{2,3},{3,4},{4,5},{5,6},{6,7},{7,8},{8,9},{9,10},{10,1... | collective-permute-start | bytes 3145736 | tf_op jit(solution)/shard_map/ppermute | solution.py:12
  7.9 16.2 %collective-permute-start.1 = (f32[1,256,1024]{2,1,0:T(8,128)S(1)}, f32[1,256,1024]{2,1,0:T(8,128)}, u32[]{:S(2)}, u32[]{:S(2)}) collective-permute-start(f32[1,256,1024]{2,1,0:T(8,128)S(1)} %get-tuple-element.200), channel_id=1, source_target_pairs={{1,0},{2,1},{3,2},{4,3},{5,4},{6,5},{7,6},{8,7},{9,8},{10,9},{11,1... | collective-permute-start | bytes 3145736 | tf_op jit(solution)/shard_map/ppermute | solution.py:15
  26.5 9.6 %copy-start.2 = (f32[2,3]{1,0:T(2,128)S(1)}, f32[2,3]{1,0:T(2,128)}, u32[]{:S(2)}) copy-start(f32[2,3]{1,0:T(2,128)} %param.6) | copy-start | bytes 76
  38.4 3.4 %copy-start = (f32[3,256,1024]{2,1,0:T(8,128)S(1)}, f32[3,256,1024]{2,1,0:T(8,128)}, u32[]{:S(2)}) copy-start(f32[3,256,1024]{2,1,0:T(8,128)} %get-tuple-element.264) | copy-start | bytes 9437188 | tf_op jit(solution)/shard_map/while
  43.8 1.7 copy-start.1
  47.9 3.4 %copy-start = (f32[3,256,1024]{2,1,0:T(8,128)S(1)}, f32[3,256,1024]{2,1,0:T(8,128)}, u32[]{:S(2)}) copy-start(f32[3,256,1024]{2,1,0:T(8,128)} %get-tuple-element.264) | copy-start | bytes 9437188 | tf_op jit(solution)/shard_map/while
  53.3 1.7 copy-start.1
  57.5 3.4 %copy-start = (f32[3,256,1024]{2,1,0:T(8,128)S(1)}, f32[3,256,1024]{2,1,0:T(8,128)}, u32[]{:S(2)}) copy-start(f32[3,256,1024]{2,1,0:T(8,128)} %get-tuple-element.264) | copy-start | bytes 9437188 | tf_op jit(solution)/shard_map/while
  62.8 1.7 copy-start.1
  67.0 3.4 %copy-start = (f32[3,256,1024]{2,1,0:T(8,128)S(1)}, f32[3,256,1024]{2,1,0:T(8,128)}, u32[]{:S(2)}) copy-start(f32[3,256,1024]{2,1,0:T(8,128)} %get-tuple-element.264) | copy-start | bytes 9437188 | tf_op jit(solution)/shard_map/while
  72.3 1.7 copy-start.1
  76.5 3.4 %copy-start = (f32[3,256,1024]{2,1,0:T(8,128)S(1)}, f32[3,256,1024]{2,1,0:T(8,128)}, u32[]{:S(2)}) copy-start(f32[3,256,1024]{2,1,0:T(8,128)} %get-tuple-element.264) | copy-start | bytes 9437188 | tf_op jit(solution)/shard_map/while
  81.8 1.7 copy-start.1
  86.0 3.4 %copy-start = (f32[3,256,1024]{2,1,0:T(8,128)S(1)}, f32[3,256,1024]{2,1,0:T(8,128)}, u32[]{:S(2)}) copy-start(f32[3,256,1024]{2,1,0:T(8,128)} %get-tuple-element.264) | copy-start | bytes 9437188 | tf_op jit(solution)/shard_map/while
  91.3 1.7 copy-start.1
  95.5 3.4 %copy-start = (f32[3,256,1024]{2,1,0:T(8,128)S(1)}, f32[3,256,1024]{2,1,0:T(8,128)}, u32[]{:S(2)}) copy-start(f32[3,256,1024]{2,1,0:T(8,128)} %get-tuple-element.264) | copy-start | bytes 9437188 | tf_op jit(solution)/shard_map/while
  100.8 1.7 copy-start.1
  105.0 3.4 %copy-start = (f32[3,256,1024]{2,1,0:T(8,128)S(1)}, f32[3,256,1024]{2,1,0:T(8,128)}, u32[]{:S(2)}) copy-start(f32[3,256,1024]{2,1,0:T(8,128)} %get-tuple-element.264) | copy-start | bytes 9437188 | tf_op jit(solution)/shard_map/while
  110.3 1.7 copy-start.1
  138.0 15.1 %all-to-all-start.1 = ((f32[1,8,8,128]{3,1,0,2:T(8,128)}), f32[1,8,8,128]{3,1,0,2:T(8,128)S(1)}, u32[]{:S(2)}, u32[]{:S(2)}) async-start(f32[1,8,8,128]{3,1,0,2:T(8,128)} %bitcast.1), calls=%async_computation.1 | async-start | bytes 65536 | tf_op jit(solution)/shard_map/all_to_all | solution.py:81
  153.0 45.9 %all-to-all-start.2 = ((f32[3,32,8,1024]{3,2,0,1:T(8,128)}), f32[3,32,8,1024]{3,2,0,1:T(8,128)}, u32[]{:S(2)}, u32[]{:S(2)}) async-start(f32[3,32,8,1024]{3,2,0,1:T(8,128)} %copy.13), calls=%async_computation.2 | async-start | bytes 6291456 | tf_op jit(solution)/shard_map/all_to_all | solution.py:70
  159.0 16.1 %copy-start.3 = (s32[8]{0:T(128)S(1)}, s32[8]{0:T(128)}, u32[]{:S(2)}) copy-start(s32[8]{0:T(128)} %param.7) | copy-start | bytes 100
  201.9 10.7 %all-to-all-start.3 = ((f32[3,8,8,128]{3,1,0,2:T(8,128)}), f32[3,8,8,128]{3,1,0,2:T(8,128)S(1)}, u32[]{:S(2)}, u32[]{:S(2)}) async-start(f32[3,8,8,128]{3,1,0,2:T(8,128)} %copy_bitcast_fusion), calls=%async_computation.3 | async-start | bytes 196608 | tf_op jit(solution)/shard_map/all_to_all | solution.py:80
where the time goes:
time: 215 us; the launch traced here: 213 us
  other arithmetic  86.1 us (40%)
  waiting for transfers between devices  47.5 us (22%)
  local copies, waits for them, and re-layouts  29.1 us (14%)
  blocking collectives  25.1 us (12%)
  starting transfers between devices  24 us (11%)
    add x16, other arithmetic, advance(): return (radiance_now + weight[None] * emitted, depth_now + optical)  27.9 us
    mul x8, other arithmetic, advance(): weight = jnp.exp(-depth_now) * -jnp.expm1(-optical)  26 us
    all_to_all x1, blocking collectives, body(): lax.all_to_all(log_trans, 'fine', split_axis=1, concat_axis=1, tiled=True)  25.1 us
    all_to_all x1, waiting for transfers between devices, body(): lax.all_to_all(radiance, 'fine', split_axis=1, concat_axis=1, tiled=True)  23.6 us
    another operation x1, other arithmetic, body(): before_sum = jnp.cumsum(got_log, axis=1) - got_log  16.1 us
    while x40, local copies, waits for them, and re-layouts  14.7 us
    ppermute x1, waiting for transfers between devices, padded_2(): lax.ppermute(lax.slice_in_dim(block, block.shape[dim] - width, None, axis...  10.1 us
    concatenate x1, other arithmetic, body(): jnp.concatenate([lower_plane[None], volume, upper_plane[None]], axis=0)  9.57 us
  transfers between devices with their start and end apart: 5, of which 5 were waited for; matrix products, arithmetic and copies ran while one was open for 10% of the time, Pallas kernels for 0%

commit v1 on v0

v1 whole, which is shorter than its diff:
```python
import functools

import jax
import jax.numpy as jnp
from jax import lax
from jax.experimental import pallas as pl
from jax.experimental.pallas import tpu as pltpu
from jax.sharding import PartitionSpec as P

MESH = pl.DeviceIdType.MESH
NX, NY, NZ = 4, 4, 8
PLANES, ROWS, COLS = 8, 256, 1024
TILES = COLS // 128
SLOTS, UNITS = 4, 16
LAG = 2


def flip1(i):
    return i + 1 - 2 * (i % 2)


def pick(base, q):
    return jnp.where(q == 0, (base + 2) % 4, jnp.where(q == 1, flip1(base), jnp.where(q == 2, 3 - base, base)))


def kernel(step_size, par, order, vol, out, buf, part, prec, rec1, rec2, x1rec, x2rec, zrec,
           edge_sem, inner_sem, fill_sem, halo_send, hl_recv, hu_recv, c_send, c_recv,
           y1_send, y1_recv, y2_send, y2_recv, x1_send, x1_recv, x2_send, x2_recv, z_send, z_recv, gossip):
    z = lax.axis_index("coarse")
    f = lax.axis_index("fine")
    x, y, c = f // 8, (f // 2) % 4, f % 2
    ring = z // 2

    def at(xx, yy, cc):
        return (z, xx * 8 + yy * 2 + cc)

    partner = at(x, y, 1 - c)
    y_pair, y_cross = at(x, flip1(y), c), at(x, 3 - y, c)
    x_pair, x_cross = at(flip1(x), y, c), at(3 - x, y, c)
    z_near = (((z + 1) % NZ, f), ((z + NZ - 1) % NZ, f))

    def signal(sem, device):
        pl.semaphore_signal(sem, inc=1, device_id=device, device_id_type=MESH)

    barrier = pltpu.get_barrier_semaphore()

    @pl.when(f > 0)
    def _():
        signal(barrier, (z, f - 1))

    @pl.when(f < 31)
    def _():
        signal(barrier, (z, f + 1))

    for device in (y_pair, y_cross, x_pair, x_cross) + z_near:
        signal(barrier, device)

    def load(first, count, j, sem):
        return pltpu.make_async_copy(
            vol.at[pl.ds(first, count), :, pl.ds(j * 128, 128)],
            buf.at[pl.ds(first + 1, count), j + 1, pl.ds(8, ROWS), :],
            sem,
        )

    for first in (0, PLANES - 1):
        for j in range(TILES):
            load(first, 1, j, edge_sem.at[(first > 0) * TILES + j]).start()
    for j in range(TILES):
        load(1, PLANES - 2, j, inner_sem.at[j]).start()
    for first in (0, PLANES - 1):
        for j in range(TILES):
            load(first, 1, j, edge_sem.at[(first > 0) * TILES + j]).wait()

    neighbours = jnp.where(f > 0, 1, 0) + jnp.where(f < 31, 1, 0)
    pl.semaphore_wait(barrier, 6 + neighbours)

    def send(src, dst, send_sem, recv_sem, device):
        return pltpu.make_async_remote_copy(
            src_ref=src, dst_ref=dst, send_sem=send_sem, recv_sem=recv_sem, device_id=device, device_id_type=MESH
        )

    def first_tile(q):
        return 2 * ((ring + 1 + q) % 4)

    body_rows = pl.ds(8, ROWS)

    def halo(src_plane, dst_plane, recv, q, device):
        tiles = pl.ds(1 + first_tile(q), 2)
        return send(
            buf.at[src_plane, tiles, body_rows, :], buf.at[dst_plane, tiles, body_rows, :], halo_send, recv.at[q], device
        )

    def halo_down(q):
        return halo(1, PLANES + 1, hu_recv, q, (z, f - 1))

    def halo_up(q):
        return halo(PLANES, 0, hl_recv, q, (z, f + 1))

    @pl.loop(0, SLOTS)
    def _(q):
        @pl.when(f > 0)
        def _():
            halo_down(q).start()

        @pl.when(f < 31)
        def _():
            halo_up(q).start()

    for device in z_near:
        signal(gossip.at[0], device)

    def fill(src, dst):
        copy = pltpu.make_async_copy(
            buf.at[src, pl.ds(1, TILES), body_rows, :], buf.at[dst, pl.ds(1, TILES), body_rows, :], fill_sem
        )
        copy.start()
        copy.wait()

    @pl.when(f == 0)
    def _():
        fill(1, 0)

    @pl.when(f == 31)
    def _():
        fill(PLANES, PLANES + 1)

    for j in range(TILES):
        load(1, PLANES - 2, j, inner_sem.at[j]).wait()

    inner = pl.ds(1, PLANES)
    buf[inner, 1 : TILES + 1, 7:8, :] = buf[inner, 1 : TILES + 1, 8:9, :]
    buf[inner, 1 : TILES + 1, ROWS + 8 : ROWS + 9, :] = buf[inner, 1 : TILES + 1, ROWS + 7 : ROWS + 8, :]

    @pl.loop(0, ROWS // 8)
    def _(i):
        rows = pl.ds(pl.multiple_of(8 + i * 8, 8), 8)
        buf[inner, 0, rows, :] = pltpu.roll(buf[inner, 1, rows, :], 127, 2)
        buf[inner, TILES + 1, rows, :] = pltpu.roll(buf[inner, TILES, rows, :], 1, 2)

    slopes = [0.5 * par[0, i] for i in range(3)]
    offsets = [0.5 * par[1, i] for i in range(3)]
    density = 0.25 * step_size

    def march(q, g):
        j = 1 + first_tile(q)
        tiles, lefts, rights = pl.ds(j, 2), pl.ds(j - 1, 2), pl.ds(j + 1, 2)
        shape = (2, 16, 128)
        lane = lax.broadcasted_iota(jnp.int32, shape, 2)
        first, last = lane == 0, lane == 127

        @pl.loop(0, 4)
        def _(i):
            row = pl.multiple_of(8 + (pick(x, i) * 4 + pick(y, g)) * 16, 8)
            rows, above, below = pl.ds(row, 16), pl.ds(row - 1, 16), pl.ds(row + 1, 16)
            previous = buf[0, tiles, rows, :]
            s = buf[1, tiles, rows, :]
            total = jnp.zeros(shape, jnp.float32)
            colours = [total] * 3
            depth, clear = total, total + 1.0
            for p in range(1, PLANES + 1):
                following = buf[p + 1, tiles, rows, :]
                left = jnp.where(last, buf[p, lefts, rows, :], s)
                right = jnp.where(first, buf[p, rights, rows, :], s)
                dz = following - previous
                dy = buf[p, tiles, below, :] - buf[p, tiles, above, :]
                dx = pltpu.roll(right, 127, 2) - pltpu.roll(left, 1, 2)
                lit = jnp.abs((dz + dx) * 0.65 + dy * 0.325)
                shading = 0.525 + lit * lax.rsqrt(dz * dz + dy * dy + (dx * dx + 4.0))
                optical = s * s * density
                alpha = optical * (1.0 + optical * (-0.5 + optical * (1.0 / 6.0 - optical * (1.0 / 24.0))))
                weight = clear * alpha
                clear = clear - weight
                depth = depth + optical
                lead = weight * shading
                total = total + lead
                for n in range(3):
                    colours[n] = colours[n] + lead * jnp.tanh(s * slopes[n] + offsets[n])
                previous, s = s, following
            values = [total + colours[n] for n in range(3)] + [depth]
            for half in range(2):
                for n in range(4):
                    part[half, q, g, i, n] = values[n][:, half * 8 : half * 8 + 8]

    def core_copy(q, g):
        return send(part.at[1 - c, q, g], prec.at[q, g], c_send, c_recv.at[q * 4 + g], partner)

    def y1_copy(q, g, i):
        return send(part.at[c, q, g, i], rec1.at[q, g, i], y1_send, y1_recv.at[(q * 2 + g) * 4 + i], y_pair)

    def y2_copy(q, i):
        return send(part.at[c, q, 2, i], rec2.at[q, i], y2_send, y2_recv.at[q * 4 + i], y_cross)

    def x1_copy(q, i):
        return send(part.at[c, q, 3, i], x1rec.at[q, i], x1_send, x1_recv.at[q * 2 + i], x_pair)

    def x2_copy(q):
        return send(part.at[c, q, 3, 2], x2rec.at[q], x2_send, x2_recv.at[q], x_cross)

    def z_copy(q, t):
        to = first_tile(q) + t
        return send(part.at[c, q, 3, 3, :, t], zrec.at[z], z_send, z_recv.at[z], (to, f))

    def z_arrival(source):
        return send(zrec.at[source], zrec.at[source], z_send, z_recv.at[source], (z, f))

    def merge(mine, theirs, behind):
        near, far = mine[3], theirs[3]
        keep = jnp.exp(-(1.0 - behind) * far)
        take = jnp.exp(-behind * near)
        for n in range(3):
            mine[n] = keep * mine[n] + take * theirs[n]
        mine[3] = near + far

    def in_front(flag):
        return flag.astype(jnp.float32)

    c_front = in_front(1 - c)
    y1_front, y2_front = in_front(1 - y % 2), in_front(1 - y // 2)
    x1_front, x2_front = in_front(1 - x % 2), in_front(1 - x // 2)

    @pl.loop(0, UNITS + LAG)
    def _(u):
        q, g = u // 4, u % 4
        v = u - LAG
        old_q, old_g = v // 4, v % 4

        @pl.when(u < UNITS)
        def _():
            @pl.when((g == 0) & (f > 0))
            def _():
                halo_up(q).wait_recv()

            @pl.when((g == 0) & (f < 31))
            def _():
                halo_down(q).wait_recv()

            march(q, g)

        @pl.when(v >= 0)
        def _():
            core_copy(old_q, old_g).wait_recv()

            @pl.loop(0, 4)
            def _(i):
                merge(part.at[c, old_q, old_g, i], prec.at[old_q, old_g, i], c_front)

        @pl.when(u < UNITS)
        def _():
            core_copy(q, g).start()

        @pl.when((v >= 0) & (old_g < 2))
        def _():
            @pl.loop(0, 4)
            def _(i):
                y1_copy(old_q, old_g, i).start()

        for level in range(2):
            @pl.when(u == 4 + 4 * level)
            def _():
                pl.semaphore_wait(gossip.at[level], 2)
                for device in z_near:
                    signal(gossip.at[level + 1], device)

    pl.semaphore_wait(gossip.at[2], 2)

    @pl.loop(0, SLOTS)
    def _(q):
        @pl.loop(0, 4)
        def _(i):
            y1_copy(q, 0, i).wait_recv()
            merge(part.at[c, q, 2, i], rec1.at[q, 0, i], y1_front)
            y2_copy(q, i).start()

        @pl.loop(0, 4)
        def _(i):
            mine = part.at[c, q, 3, i]
            y1_copy(q, 1, i).wait_recv()
            merge(mine, rec1.at[q, 1, i], y1_front)
            y2_copy(q, i).wait_recv()
            merge(mine, rec2.at[q, i], y2_front)

            @pl.when(i < 2)
            def _():
                x1_copy(q, i).start()

            @pl.when(i >= 2)
            def _():
                x1_copy(q, i - 2).wait_recv()
                merge(mine, x1rec.at[q, i - 2], x1_front)

            @pl.when(i == 2)
            def _():
                x2_copy(q).start()

            @pl.when(i == 3)
            def _():
                x2_copy(q).wait_recv()
                merge(mine, x2rec.at[q], x2_front)

        for t in range(2):
            @pl.when((q < SLOTS - 1) | (z % 2 != t))
            def _():
                z_copy(q, t).start()

    zrec[z] = part[c, SLOTS - 1, 3, 3, :, z % 2]

    halo_rows = buf.at[0, pl.ds(1, TILES), body_rows, :]

    @pl.when(f > 0)
    def _():
        send(halo_rows, halo_rows, halo_send, hl_recv.at[0], partner).wait_send()

    @pl.when(f < 31)
    def _():
        send(halo_rows, halo_rows, halo_send, hl_recv.at[0], partner).wait_send()

    send(prec, prec, c_send, c_recv.at[0], partner).wait_send()
    send(rec1, rec1, y1_send, y1_recv.at[0], y_pair).wait_send()
    send(rec2, rec2, y2_send, y2_recv.at[0], y_cross).wait_send()
    send(x1rec, x1rec, x1_send, x1_recv.at[0], x_pair).wait_send()
    send(x2rec, x2rec, x2_send, x2_recv.at[0], x_cross).wait_send()

    for step in range(1, NZ):
        z_arrival((z + step) % NZ).wait_recv()

    depths = [zrec[g, 3] for g in range(NZ)]
    image = [jnp.zeros((8, 128), jnp.float32)] * 3
    whole = jnp.zeros((8, 128), jnp.float32)
    for g in range(NZ):
        before = jnp.zeros((8, 128), jnp.float32)
        for h in range(NZ):
            if h != g:
                before = before + depths[h] * (order[h] < order[g]).astype(jnp.float32)
        through = jnp.exp(-before)
        for n in range(3):
            image[n] = image[n] + through * zrec[g, n]
        whole = whole + depths[g]
    for n in range(3):
        out[n] = image[n]
    out[3] = whole
    seven = zrec.at[pl.ds(0, NZ - 1)]
    send(seven, seven, z_send, z_recv.at[0], z_near[0]).wait_send()


def finish(done, img, opa):
    img[...] = done[:3]
    whole = done[3]
    tail = 1.0 - whole * (1.0 / 6.0)
    for n in (5, 4, 3, 2):
        tail = 1.0 - whole * (1.0 / n) * tail
    opa[...] = jnp.where(whole < 0.25, whole * tail, 1.0 - jnp.exp(-whole))


def body(volume, color_params, depth_order):
    cell = (4, 2, 8, 128)
    dma = pltpu.SemaphoreType.DMA
    step_size = 4.0 / (PLANES * NX * NY * 2 * NZ)
    done = pl.pallas_call(
        functools.partial(kernel, step_size),
        out_shape=jax.ShapeDtypeStruct((4, 8, 128), jnp.float32),
        in_specs=[
            pl.BlockSpec(memory_space=pltpu.SMEM),
            pl.BlockSpec(memory_space=pltpu.SMEM),
            pl.BlockSpec(memory_space=pl.ANY),
        ],
        out_specs=pl.BlockSpec(memory_space=pltpu.VMEM),
        scratch_shapes=[
            pltpu.VMEM((PLANES + 2, TILES + 2, ROWS + 16, 128), jnp.float32),
            pltpu.VMEM((2, SLOTS, 4, 4) + cell, jnp.float32),
            pltpu.VMEM((SLOTS, 4, 4) + cell, jnp.float32),
            pltpu.VMEM((SLOTS, 2, 4) + cell, jnp.float32),
            pltpu.VMEM((SLOTS, 4) + cell, jnp.float32),
            pltpu.VMEM((SLOTS, 2) + cell, jnp.float32),
            pltpu.VMEM((SLOTS,) + cell, jnp.float32),
            pltpu.VMEM((NZ, 4, 8, 128), jnp.float32),
            dma((2 * TILES,)), dma((TILES,)), dma,
            dma, dma((SLOTS,)), dma((SLOTS,)),
            dma, dma((UNITS,)),
            dma, dma((2 * UNITS,)), dma, dma((UNITS,)),
            dma, dma((2 * SLOTS,)), dma, dma((SLOTS,)),
            dma, dma((NZ,)),
            pltpu.SemaphoreType.REGULAR((3,)),
        ],
        compiler_params=pltpu.CompilerParams(collective_id=0, has_side_effects=True),
    )(color_params, depth_order, volume)

    return pl.pallas_call(
        finish,
        out_shape=(jax.ShapeDtypeStruct((3, 8, 128), jnp.float32), jax.ShapeDtypeStruct((8, 128), jnp.float32)),
    )(done)


def solution(mesh):
    return jax.shard_map(
        body,
        mesh=mesh,
        in_specs=(P(("coarse", "fine"), None, None), P(), P()),
        out_specs=(P(None, "fine", "coarse"), P("fine", "coarse")),
        check_vma=False,
    )
```

time: 215 us -> 76.8 us (0.36)
  the two profiles are of different devices: /device:TPU:1 before, /device:TPU:36 now
where the time goes in v1:
time: 76.8 us; the launch traced here: 76.6 us
  Pallas kernels  75.9 us (99%)
    pallas_call x1, Pallas kernels, body(): pl.pallas_call(functools.partial(kernel, step_size), out_shape=jax.ShapeD...  74.6 us

profile of v1, /device:TPU:36, one launch (start us, length us, event | category | flops | bytes accessed | tf_op | source)
XLA Modules:
  0.0 76.6 jit_solution(8812457005264493462)
XLA Ops:
  0.6 74.6 %shard_map.50.done = f32[4,8,128]{2,1,0:T(8,128)} custom-call(f32[2,3]{1,0:T(2,128)} %par.1, s32[8]{0:T(128)} %order.1, f32[8,256,1024]{2,1,0:T(8,128)} %vol.1), custom_call_target="tpu_custom_call" | custom-call | tf_op jit(solution)/shard_map/pallas_call | solution.py:358
  75.2 1.3 %shard_map.51 = (f32[3,8,128]{2,1,0:T(8,128)}, f32[8,128]{1,0:T(8,128)}) custom-call(f32[4,8,128]{2,1,0:T(8,128)} %shard_map.50.done), custom_call_target="tpu_custom_call" | custom-call | tf_op jit(solution)/shard_map/pallas_call | solution.py:387
